TPU v7x, 256 devices: a whole 4x4x8 slice. The times are simulated.
256 devices in a mesh: gz: 16 (over y, x), dom: 16 (over z, core).
Axes of the slice: x: 4, y: 4, z: 8, core: 2. Of those that a mesh axis runs over, the one named last changes fastest.
Arguments:
- volume: float32 [768, 4, 384], P('gz'), may hold values from -6 to 6
- observed: bfloat16 [4096, 4, 384], P(('gz', 'dom')), may hold values from -6 to 6
- ctf_table: float32 [32, 2, 384], replicated, may hold values from -1 to 1
- ctf_class: int32 [4096], P(('gz', 'dom')), may hold values from 0 to 31
- bin_ids: int32 [4096], P(('gz', 'dom')), may hold values from 0 to 127
Outputs:
- pose_score: float32 [4096], P(('gz', 'dom'))
- backprojection: float32 [768, 4, 384], P(('gz', 'dom'))
All inputs are finite; a program needn't handle non-finite values.
Results may differ from a plain program's by a relative error of at most 0.0034.
Values may be sent and summed in bfloat16 or wider, within the bound.
A program may use at most 64 MiB of HBM per device.

v0:
```python
import math
import jax
import jax.numpy as jnp
from jax import lax
from jax.sharding import PartitionSpec as P

NZ = 768
NB_DEV = 8
NCTF = 32
ITERS = 3
epsilon = 1e-05


def kernel(offset):
    inside = jnp.abs(offset) < 1.0
    falloff = 1.0 - offset * offset
    return (
        jnp.where(inside, falloff * falloff, 0.0),
        jnp.where(inside, -4.0 * offset * falloff, 0.0),
    )


def geometry(bin_index, planes, total_bins, samples, columns):
    tilt_angle = -0.5 * math.pi + math.pi * (bin_index.astype(jnp.float32) + 0.5) / total_bins
    sine_value = jnp.sin(tilt_angle)
    cosine = jnp.cos(tilt_angle)
    radius = jnp.arange(samples).astype(jnp.float32)
    centre = 0.5 * NZ + radius * sine_value
    z_value, z_slope = kernel(planes[None, :] - centre[:, None])
    z_slope = z_slope * (-radius * cosine / samples)[:, None]
    x_value, x_slope = kernel(
        jnp.arange(columns).astype(jnp.float32)[None, :] - (radius * cosine)[:, None]
    )
    x_slope = x_slope * (radius * sine_value / samples)[:, None]
    return (z_value, z_slope, jnp.concatenate([x_value, x_slope], 0))


def contrast_of(classes, ctf_table, count, stacked_rows, samples):
    class_onehot = (classes[:, None] == jnp.arange(NCTF, dtype=jnp.int32)[None, :]).astype(
        jnp.float32
    )
    contrast = jnp.dot(
        class_onehot,
        ctf_table.reshape(NCTF, -1),
        precision=lax.Precision.HIGHEST,
        preferred_element_type=jnp.float32,
    )
    contrast = contrast.reshape(count, stacked_rows // 2, samples)
    return jnp.concatenate([contrast, contrast], 1)


def local(volume, observed, ctf_table, ctf_class, bin_ids):
    depth_local = volume.shape[0]
    stacked_rows = volume.shape[1]
    columns = volume.shape[2]
    samples = observed.shape[2]
    particles = observed.shape[0]
    total_bins = NB_DEV * lax.axis_size("dom")
    first_bin = lax.axis_index("dom") * NB_DEV
    planes = (lax.axis_index("gz") * depth_local + jnp.arange(depth_local, dtype=jnp.int32)).astype(
        jnp.float32
    )
    flat_volume = volume.reshape(depth_local * stacked_rows, columns)

    def extract(offset):
        z_value, z_slope, x_weights = geometry(
            first_bin + offset, planes, total_bins, samples, columns
        )
        resampled = jnp.dot(
            flat_volume,
            x_weights.T,
            precision=lax.Precision.HIGHEST,
            preferred_element_type=jnp.float32,
        )
        resampled = resampled.reshape(depth_local, stacked_rows, 2 * samples)
        direct = resampled[:, :, :samples]
        tilted = resampled[:, :, samples:]
        leading = jnp.sum(direct * z_value.T[:, None, :], axis=0)
        second = jnp.sum(direct * z_slope.T[:, None, :] + tilted * z_value.T[:, None, :], axis=0)
        return jnp.concatenate([leading, second], 0)

    partial_slices = lax.map(extract, jnp.arange(NB_DEV, dtype=jnp.int32))
    reduced = lax.psum(partial_slices, "gz")
    gathered = lax.all_gather(reduced.astype(jnp.bfloat16), "dom", axis=0, tiled=True)
    bin_onehot = bin_ids[:, None] == jnp.arange(total_bins, dtype=jnp.int32)[None, :]
    picked = jnp.dot(
        bin_onehot.astype(jnp.bfloat16),
        gathered.reshape(total_bins, -1),
        preferred_element_type=jnp.float32,
    )
    picked = picked.reshape(particles, 2 * stacked_rows, samples)
    contrast = contrast_of(ctf_class, ctf_table, particles, stacked_rows, samples)
    measured = observed.astype(jnp.float32)
    predicted = contrast * picked[:, :stacked_rows]
    tangent = contrast * picked[:, stacked_rows:]
    curvature = jnp.sum(tangent * tangent, axis=(1, 2)) + epsilon
    shift = jnp.zeros((particles,), jnp.float32)
    for iteration in range(ITERS):
        residual_map = measured - predicted - shift[:, None, None] * tangent
        shift = shift + 0.5 * jnp.sum(residual_map * tangent, axis=(1, 2)) / curvature
    pose_score = shift * jnp.sqrt(curvature)
    onehot_float = bin_onehot.astype(jnp.float32)
    weighted = contrast * measured
    contributions = jnp.concatenate([weighted, shift[:, None, None] * weighted], 1).reshape(
        particles, -1
    )
    totals = jnp.dot(
        onehot_float.T,
        contributions,
        precision=lax.Precision.HIGHEST,
        preferred_element_type=jnp.float32,
    )
    totals = lax.psum(totals, ("gz", "dom"))
    owned = lax.dynamic_slice_in_dim(totals, first_bin, NB_DEV, 0)
    owned = owned.reshape(NB_DEV, 2 * stacked_rows, samples)

    def spread_back(offset, accumulated):
        z_value, z_slope, x_weights = geometry(
            first_bin + offset, planes, total_bins, samples, columns
        )
        summed = lax.dynamic_index_in_dim(owned, offset, 0, keepdims=False)
        direct = summed[:stacked_rows]
        tilted = summed[stacked_rows:]
        z_plain = z_value.T[:, None, :]
        z_tilted = z_slope.T[:, None, :]
        leading = z_plain * direct[None] + z_tilted * tilted[None]
        second = z_plain * tilted[None]
        stacked = jnp.concatenate([leading, second], 2).reshape(
            depth_local * stacked_rows, 2 * samples
        )
        return accumulated + jnp.dot(
            stacked, x_weights, precision=lax.Precision.HIGHEST, preferred_element_type=jnp.float32
        )

    backprojected = lax.fori_loop(
        0, NB_DEV, spread_back, jnp.zeros((depth_local * stacked_rows, columns), jnp.float32)
    )
    backprojected = backprojected.reshape(depth_local, stacked_rows, columns)
    plane_share = lax.psum_scatter(backprojected, "dom", scatter_dimension=0, tiled=True)
    return (pose_score, plane_share)


def solution(mesh):
    return jax.shard_map(
        local,
        mesh=mesh,
        in_specs=(
            P("gz", None, None),
            P(("gz", "dom"), None, None),
            P(),
            P(("gz", "dom")),
            P(("gz", "dom")),
        ),
        out_specs=(P(("gz", "dom")), P(("gz", "dom"), None, None)),
        check_vma=False,
    )
```

profile of v0, /device:TPU:1, one launch (start us, length us, event | category | flops | bytes accessed | tf_op | source)
XLA Modules:
  0.0 525.4 jit_solution(10506065352268123500)
XLA Ops:
  8.3 28.8 %while.29 = (s32[]{:T(128)}, f32[8,8,384]{2,1,0:T(8,128)S(1)}, s32[8]{0:T(128)S(1)}, s32[]{:T(128)}, f32[192,384]{1,0:T(8,128)S(1)}, /*index=5*/s32[]{:T(128)}, s32[]{:T(128)}, f32[]{:T(128)}, f32[]{:T(128)}, f32[]{:T(128)}) while((s32[]{:T(128)}, f32[8,8,384]{2,1,0:T(8,128)S(1)}, s32[8]{0:T(128)S(1)}, s32[]{:T(128)}, ...), condition=%wide.region_3.4_spmd.clone, body=%wide.region_0.3_spmd.clone.sunk | while | flops 682043264 | bytes 5361225 | solution.py:82
  10.0 1.4 convolution_bitcast_fusion.2
  13.5 1.5 convolution_bitcast_fusion.2
  17.2 1.4 convolution_bitcast_fusion.2
  20.7 1.5 convolution_bitcast_fusion.2
  24.4 1.4 convolution_bitcast_fusion.2
  28.0 1.5 convolution_bitcast_fusion.2
  31.6 1.4 convolution_bitcast_fusion.2
  35.2 1.5 convolution_bitcast_fusion.2
  37.2 62.0 %psum.14 = bf16[8,8,384]{2,1,0:T(8,128)(2,1)S(1)} all-reduce(f32[8,8,384]{2,1,0:T(8,128)S(1)} %get-tuple-element.211), channel_id=1, replica_groups=mesh['gz'=16,'dom'=16] {'gz'}, use_global_device_ids=true, to_apply=%region_4.5 | all-reduce | flops 24576 | bytes 147456 | tf_op jit(solution)/shard_map/psum | solution.py:83
  99.1 36.8 %all_gather.3 = bf16[128,8,384]{2,1,0:T(8,128)(2,1)S(1)} all-gather(bf16[8,8,384]{2,1,0:T(8,128)(2,1)S(1)} %psum.14), channel_id=1, replica_groups=mesh['gz'=16,'dom'=16] {'dom'}, dimensions={0}, use_global_device_ids=true | all-gather | bytes 835584 | tf_op jit(solution)/shard_map/all_gather | solution.py:84
  138.4 2.0 fusion.63
  140.5 251.3 %all-reduce.4.cloned.1.call-done = f32[128,3072]{1,0:T(8,128)} async-done(((f32[128,3072]{1,0:T(8,128)}), f32[128,3072]{1,0:T(8,128)}) %all-reduce.4.cloned.1.call-update) | async-done | bytes 1572880 | tf_op jit(solution)/shard_map/psum | solution.py:113
  392.7 17.9 %while.30 = (s32[]{:T(128)}, f32[192,384]{1,0:T(8,128)S(1)}, s32[]{:T(128)}, f32[8,8,384]{2,1,0:T(8,128)S(1)}, s32[]{:T(128)}, /*index=5*/s32[]{:T(128)}, f32[]{...) while((s32[]{:T(128)}, f32[192,384]{1,0:T(8,128)S(1)}, s32[]{:T(128)}, ...), condition=%wide.region_11.12_spmd.clone, body=%wide.region_10.11_spmd.clone.sunk | while | flops 682190720 | bytes 5656159 | solution.py:135
  393.7 1.2 fusion.96
  395.9 1.2 fusion.96
  398.2 1.2 fusion.96
  400.4 1.2 fusion.96
  402.6 1.2 fusion.96
  404.9 1.2 fusion.96
  407.1 1.2 fusion.96
  409.4 1.2 fusion.96
  412.7 104.5 %all-reduce.6.cloned.1.call-done = f32[48,4,384]{2,1,0:T(4,128)} async-done(((f32[48,4,384]{2,1,0:T(4,128)}), f32[48,4,384]{2,1,0:T(4,128)}) %all-reduce.6.cloned.1.call-update) | async-done | bytes 294928
  517.2 1.3 constant_dynamic-slice_fusion
  (194 shorter events, 22.5 us)
Async XLA Ops:
  7.2 384.6 %all-reduce.4.cloned.1.call-start = ((), (), s32[]{:S(2)}) async-start(), calls=%async_computation | async-start | bytes 3145728 | tf_op jit(solution)/shard_map/psum | solution.py:113
  99.1 37.5 %copy-start.2 = (s32[16]{0:T(128)S(1)}, s32[16]{0:T(128)}, u32[]{:S(2)}) copy-start(s32[16]{0:T(128)} %param.13) | copy-start | bytes 196
  136.0 0.9 copy-start.1
  136.0 1.0 copy-start.3
  136.0 1.2 copy-start
  140.4 376.8 %all-reduce.6.cloned.1.call-start = ((), (), s32[]{:S(2)}) async-start(), calls=%async_computation.1 | async-start | bytes 589824
  392.7 18.7 %copy-start.4 = (u32[256]{0:T(256)S(1)}, u32[256]{0:T(256)}, u32[]{:S(2)}) copy-start(u32[256]{0:T(256)} %constant.211) | copy-start | bytes 3076
Sparse Core Ops, SparseCore 0:
  140.6 251.1 all-reduce.3
  411.6 105.6 all-reduce.5
where the time goes:
time: 526 us; the launch traced here: 525 us
  waiting for transfers between devices  356 us (68%)
  blocking collectives  98.8 us (19%)
  matrix products  24.2 us (5%)
  between operations  14.8 us (3%)
  local copies, waits for them, and re-layouts  13.1 us (2%)
  other arithmetic  10.1 us (2%)
  loops' own time  8.51 us (2%)
    psum x1, waiting for transfers between devices, local(): totals = lax.psum(totals, ('gz', 'dom'))  251 us
    unnamed x3, waiting for transfers between devices  105 us
    psum x1, blocking collectives, local(): reduced = lax.psum(partial_slices, 'gz')  62 us
    all_gather x1, blocking collectives, local(): lax.all_gather(reduced.astype(jnp.bfloat16), 'dom', axis=0, tiled=True)  36.8 us
    dot_general x8, matrix products, extract(): jnp.dot(flat_volume, x_weights.T, precision=lax.Precision.HIGHEST, prefer...  11.7 us
  transfers between devices with their start and end apart: 2, of which 2 were waited for; matrix products, arithmetic and copies ran while one was open for 0% of the time, Pallas kernels for 0%

commit v1 on v0

--- a/solution.py
+++ b/solution.py
@@ -9,6 +9,11 @@
 NCTF = 32
 ITERS = 3
 epsilon = 1e-05
+
+
+def add_all(shard, axis):
+    blocks = lax.all_gather(shard, axis)
+    return jnp.sum(blocks, axis=0)
 
 
 def kernel(offset):
@@ -80,7 +85,7 @@
         return jnp.concatenate([leading, second], 0)
 
     partial_slices = lax.map(extract, jnp.arange(NB_DEV, dtype=jnp.int32))
-    reduced = lax.psum(partial_slices, "gz")
+    reduced = add_all(partial_slices, "gz")
     gathered = lax.all_gather(reduced.astype(jnp.bfloat16), "dom", axis=0, tiled=True)
     bin_onehot = bin_ids[:, None] == jnp.arange(total_bins, dtype=jnp.int32)[None, :]
     picked = jnp.dot(

time: 526 us -> 505 us (0.960)
  blocking collectives: 98.8 us -> 21 us
  waiting for transfers between devices: 356 us -> 410 us
    psum x1 -> x0, blocking collectives: 62 us -> none  [local(): reduced = lax.psum(partial_slices, 'gz')]
    all_gather x0 -> x1, waiting for transfers between devices: none -> 51.7 us  [add_all(): blocks = lax.all_gather(shard, axis)]
    all_gather x1, blocking collectives: 36.8 us -> 21 us  [local(): lax.all_gather(reduced.astype(jnp.bfloat16), 'dom', axis=0, tiled=True)]
    unnamed x3 -> x4, waiting for transfers between devices: 105 us -> 105 us
  transfers between devices with their start and end apart: 2 -> 3, of which waited for: 2 -> 3; matrix products, arithmetic and copies ran while one was open for 0% -> 0% of each run, Pallas kernels for 0% -> 0%
where the time goes in v1:
time: 505 us; the launch traced here: 504 us
  waiting for transfers between devices  410 us (81%)
  matrix products  24 us (5%)
  blocking collectives  21 us (4%)
  between operations  14.6 us (3%)
  local copies, waits for them, and re-layouts  13.8 us (3%)
  other arithmetic  11.6 us (2%)
  loops' own time  8.98 us (2%)
    psum x1, waiting for transfers between devices, local(): totals = lax.psum(totals, ('gz', 'dom'))  254 us
    unnamed x4, waiting for transfers between devices  105 us
    all_gather x1, waiting for transfers between devices, add_all(): blocks = lax.all_gather(shard, axis)  51.7 us
    all_gather x1, blocking collectives, local(): lax.all_gather(reduced.astype(jnp.bfloat16), 'dom', axis=0, tiled=True)  21 us
    dot_general x8, matrix products, extract(): jnp.dot(flat_volume, x_weights.T, precision=lax.Precision.HIGHEST, prefer...  11.5 us
  transfers between devices with their start and end apart: 3, of which 3 were waited for; matrix products, arithmetic and copies ran while one was open for 0% of the time, Pallas kernels for 0%

profile of v1, /device:TPU:1, one launch (start us, length us, event | category | flops | bytes accessed | tf_op | source)
XLA Modules:
  0.0 504.4 jit_solution(17906692954603817963)
XLA Ops:
  8.3 29.3 %while.29 = (s32[]{:T(128)}, f32[8,8,384]{2,1,0:T(8,128)S(1)}, s32[8]{0:T(128)S(1)}, s32[]{:T(128)}, f32[192,384]{1,0:T(8,128)S(1)}, /*index=5*/s32[]{:T(128)}, s32[]{:T(128)}, f32[]{:T(128)}, f32[]{:T(128)}, f32[]{:T(128)}) while((s32[]{:T(128)}, f32[8,8,384]{2,1,0:T(8,128)S(1)}, s32[8]{0:T(128)S(1)}, s32[]{:T(128)}, ...), condition=%wide.region_3.4_spmd.clone, body=%wide.region_0.3_spmd.clone.sunk | while | flops 682043264 | bytes 5361225 | solution.py:87
  10.1 1.4 convolution_bitcast_fusion.2
  13.7 1.5 convolution_bitcast_fusion.2
  17.4 1.4 convolution_bitcast_fusion.2
  21.1 1.4 convolution_bitcast_fusion.2
  24.7 1.4 convolution_bitcast_fusion.2
  28.4 1.4 convolution_bitcast_fusion.2
  32.0 1.4 convolution_bitcast_fusion.2
  35.7 1.4 convolution_bitcast_fusion.2
  38.5 51.7 %all-gather.3.cloned.1.call-done = f32[128,8,384]{2,1,0:T(8,128)} async-done(((f32[8,8,384]{2,1,0:T(8,128)}), f32[128,8,384]{2,1,0:T(8,128)}) %all-gather.3.cloned.1.call-update) | async-done | bytes 1572880 | tf_op jit(solution)/shard_map/all_gather | solution.py:15
  90.2 1.5 reduce_sum.69
  91.7 21.0 %all_gather.11 = bf16[128,8,384]{2,1,0:T(8,128)(2,1)S(1)} all-gather(bf16[8,8,384]{2,1,0:T(8,128)(2,1)S(1)} %reduce_sum.69), channel_id=1, replica_groups=mesh['gz'=16,'dom'=16] {'dom'}, dimensions={0}, use_global_device_ids=true | all-gather | bytes 835584 | tf_op jit(solution)/shard_map/all_gather | solution.py:89
  115.0 2.0 fusion.63
  117.1 254.0 %all-reduce.4.cloned.1.call-done = f32[128,3072]{1,0:T(8,128)} async-done(((f32[128,3072]{1,0:T(8,128)}), f32[128,3072]{1,0:T(8,128)}) %all-reduce.4.cloned.1.call-update) | async-done | bytes 1572880 | tf_op jit(solution)/shard_map/psum | solution.py:118
  372.0 17.9 %while.30 = (s32[]{:T(128)}, f32[192,384]{1,0:T(8,128)S(1)}, s32[]{:T(128)}, f32[8,8,384]{2,1,0:T(8,128)S(1)}, s32[]{:T(128)}, /*index=5*/s32[]{:T(128)}, f32[]{...) while((s32[]{:T(128)}, f32[192,384]{1,0:T(8,128)S(1)}, s32[]{:T(128)}, ...), condition=%wide.region_11.12_spmd.clone, body=%wide.region_10.11_spmd.clone.sunk | while | flops 682190720 | bytes 5656159 | solution.py:140
  373.0 1.2 fusion.96
  375.3 1.2 fusion.96
  377.5 1.2 fusion.96
  379.7 1.2 fusion.96
  384.2 1.2 fusion.96
  386.5 1.2 fusion.96
  388.7 1.2 fusion.96
  392.0 104.5 %all-reduce.6.cloned.1.call-done = f32[48,4,384]{2,1,0:T(4,128)} async-done(((f32[48,4,384]{2,1,0:T(4,128)}), f32[48,4,384]{2,1,0:T(4,128)}) %all-reduce.6.cloned.1.call-update) | async-done | bytes 294928
  496.6 1.3 constant_dynamic-slice_fusion
  (199 shorter events, 24.5 us)
Async XLA Ops:
  7.2 83.1 %all-gather.3.cloned.1.call-start = ((), (), s32[]{:S(2)}) async-start(), calls=%async_computation.1 | async-start | bytes 1671168 | tf_op jit(solution)/shard_map/all_gather | solution.py:15
  8.3 30.0 %copy-start.1 = (f32[32,2,384]{2,1,0:T(2,128)S(1)}, f32[32,2,384]{2,1,0:T(2,128)}, u32[]{:S(2)}) copy-start(f32[32,2,384]{2,1,0:T(2,128)} %param.11) | copy-start | bytes 294916
  8.3 30.0 %copy-start.4 = (s32[16]{0:T(128)S(1)}, s32[16]{0:T(128)}, u32[]{:S(2)}) copy-start(s32[16]{0:T(128)} %param.12) | copy-start | bytes 196
  37.6 0.6 copy-start.2
  38.3 332.9 %all-reduce.4.cloned.1.call-start = ((), (), s32[]{:S(2)}) async-start(), calls=%async_computation | async-start | bytes 3145728 | tf_op jit(solution)/shard_map/psum | solution.py:118
  91.7 21.6 %copy-start.3 = (s32[16]{0:T(128)S(1)}, s32[16]{0:T(128)}, u32[]{:S(2)}) copy-start(s32[16]{0:T(128)} %param.13) | copy-start | bytes 196
  112.8 0.9 copy-start
  117.0 379.5 %all-reduce.6.cloned.1.call-start = ((), (), s32[]{:S(2)}) async-start(), calls=%async_computation.2 | async-start | bytes 589824
  372.0 18.8 %copy-start.5 = (u32[256]{0:T(256)S(1)}, u32[256]{0:T(256)}, u32[]{:S(2)}) copy-start(u32[256]{0:T(256)} %constant.211) | copy-start | bytes 3076
Sparse Core Ops, SparseCore 0:
  38.4 51.8 all-gather.2
  117.2 253.9 all-reduce.3
  390.9 105.6 all-reduce.5
